TPU v7x, 32 devices: a whole 2x2x4 slice. The times are simulated.
32 devices in a mesh: row: 16 (over z, y, core), col: 2 (over x).
Axes of the slice: x: 2, y: 2, z: 4, core: 2. Of those that a mesh axis runs over, the one named last changes fastest.
Arguments:
- pair: bfloat16 [384, 384, 128], P('row', 'col'), may hold values from -6 to 6
- gain: float32 [128], replicated, may hold values from 0.1 to 1.9
- projections: bfloat16 [5, 128, 128], replicated, may hold values from -0.5 to 0.5
- bias_weight: bfloat16 [128, 4], replicated, as said below
- valid_len: int32 [1], replicated, may hold values from 192 to 384
- out_cotangent: bfloat16 [384, 384, 128], P('row', 'col'), may hold values from -6 to 6
Outputs:
- attended: bfloat16 [384, 384, 128], P('row', 'col')
- pair_gradient: float32 [384, 384, 128], P('row', 'col')
- projection_grad: float32 [5, 128, 128], replicated
- bias_weight_grad: float32 [128, 4], replicated
- gain_gradient: float32 [128], replicated
Inputs may be any that keep to these rules, and one draw needn't show every extreme that they name: `bias_weight`: scale of the bias projection entries is free; rows are drawn independently.
All inputs are finite; a program needn't handle non-finite values.
Results may differ from a plain program's by a relative error of at most 0.0045.
The roundings to bfloat16 on the way count: a program that leaves them out, or rounds other values in their place, can miss the bound.
Values may be sent and summed in bfloat16 or wider, within the bound.
A program may use at most 64 MiB of HBM per device.

v0:
```python
import jax
import jax.numpy as jnp
from jax import lax
from jax.sharding import PartitionSpec as P

QB = 384


EPS = 1e-05


def dense(left, right):
    return jnp.einsum("abc,cd->abd", left, right, preferred_element_type=jnp.float32)


def outer_sum(left, right):
    return jnp.einsum("abc,abd->cd", left, right, preferred_element_type=jnp.float32)


def attend_forward(query, key, value, bias_blocks, keep):
    ncols, rows, heads, width = query.shape
    nblocks = bias_blocks.shape[0]
    scale = width ** (-0.5)

    def per_column(cols):
        qcol, kcol, vcol = cols

        def per_block(blk):
            qblk, bblk = blk
            scores = (
                jnp.einsum("qhd,khd->hqk", qblk, kcol, preferred_element_type=jnp.float32) * scale
                + bblk
            )
            scores = jnp.where(keep[None, None, :], scores, -1000000000.0)
            probs = jax.nn.softmax(scores, axis=-1)
            out = jnp.einsum(
                "hqk,khd->qhd", probs.astype(jnp.bfloat16), vcol, preferred_element_type=jnp.float32
            )
            return out.astype(jnp.bfloat16)

        return lax.map(
            per_block, (qcol.reshape(nblocks, rows // nblocks, heads, width), bias_blocks)
        ).reshape(rows, heads, width)

    return lax.map(per_column, (query, key, value))


def attend_backward(query, key, value, d_context, bias_blocks, keep):
    ncols, rows, heads, width = query.shape
    nblocks = bias_blocks.shape[0]
    qsize = rows // nblocks
    scale = width ** (-0.5)

    def per_column(total, cols):
        qcol, kcol, vcol, dcol = cols

        def per_block(carry, blk):
            dk_acc, dv_acc = carry
            qblk, dblk, bblk = blk
            scores = (
                jnp.einsum("qhd,khd->hqk", qblk, kcol, preferred_element_type=jnp.float32) * scale
                + bblk
            )
            scores = jnp.where(keep[None, None, :], scores, -1000000000.0)
            probs = jax.nn.softmax(scores, axis=-1)
            weights_b = probs.astype(jnp.bfloat16)
            d_probs = jnp.einsum("qhd,khd->hqk", dblk, vcol, preferred_element_type=jnp.float32)
            d_scores = probs * (d_probs - jnp.sum(probs * d_probs, axis=-1, keepdims=True))
            dsb = d_scores.astype(jnp.bfloat16)
            dq = (
                jnp.einsum("hqk,khd->qhd", dsb, kcol, preferred_element_type=jnp.float32) * scale
            ).astype(jnp.bfloat16)
            dk_acc = (
                dk_acc
                + jnp.einsum("hqk,qhd->khd", dsb, qblk, preferred_element_type=jnp.float32) * scale
            )
            dv_acc = dv_acc + jnp.einsum(
                "hqk,qhd->khd", weights_b, dblk, preferred_element_type=jnp.float32
            )
            return ((dk_acc, dv_acc), (dq, d_scores))

        zeros = jnp.zeros((rows, heads, width), jnp.float32)
        (dk, dv), (dq, dscores) = lax.scan(
            per_block,
            (zeros, zeros),
            (
                qcol.reshape(nblocks, qsize, heads, width),
                dcol.reshape(nblocks, qsize, heads, width),
                bias_blocks,
            ),
        )
        return (
            total + dscores,
            (dq.reshape(rows, heads, width), dk.astype(jnp.bfloat16), dv.astype(jnp.bfloat16)),
        )

    start = jnp.zeros(bias_blocks.shape, jnp.float32)
    total, (dq, dk, dv) = lax.scan(per_column, start, (query, key, value, d_context))
    return (dq, dk, dv, total)


def arrange_bias(gathered, n_row, n_col, rows):
    heads, tile_rows, tile_cols = (gathered.shape[1], gathered.shape[2], gathered.shape[3])
    grid = gathered.reshape(n_row, n_col, heads, tile_rows, tile_cols)
    bias_t = jnp.transpose(grid, (2, 1, 4, 0, 3)).reshape(heads, rows, rows)
    return bias_t.reshape(heads, rows // QB, QB, rows).transpose(1, 0, 2, 3)


def shards(pair, gain, projections, bias_weight, valid_len, out_cotangent):
    n_row = lax.axis_size("row")
    n_col = lax.axis_size("col")
    tile_rows, tile_cols, channels = pair.shape
    rows = tile_rows * n_row
    heads = bias_weight.shape[1]
    width = channels // heads
    ncols = tile_cols // n_row
    pair_float = pair.astype(jnp.float32)
    average_value = jnp.mean(pair_float, axis=-1, keepdims=True)
    var = jnp.mean((pair_float - average_value) ** 2, axis=-1, keepdims=True)
    inverse_deviation = lax.rsqrt(var + EPS)
    centered_scaled = (pair_float - average_value) * inverse_deviation
    normalized_pair = (centered_scaled * gain).astype(jnp.bfloat16)
    bias_tile = jnp.einsum(
        "abc,ch->hab", normalized_pair, bias_weight, preferred_element_type=jnp.float32
    )
    gathered = lax.all_gather(bias_tile[None], ("row", "col"), axis=0, tiled=True)
    bias_blocks = arrange_bias(gathered, n_row, n_col, rows)
    keep = jnp.arange(rows, dtype=jnp.int32) < valid_len[0]

    def split(tensor):
        return jnp.moveaxis(tensor, 1, 0).reshape(ncols, rows, heads, width)

    def join(tensor):
        return jnp.moveaxis(tensor.reshape(ncols, rows, channels), 0, 1)

    normed_cols, cot_cols = (
        lax.all_to_all(normalized_pair, "row", split_axis=1, concat_axis=0, tiled=True),
        lax.all_to_all(out_cotangent, "row", split_axis=1, concat_axis=0, tiled=True),
    )
    query = dense(normed_cols, projections[0]).astype(jnp.bfloat16)
    key = dense(normed_cols, projections[1]).astype(jnp.bfloat16)
    value = dense(normed_cols, projections[2]).astype(jnp.bfloat16)
    gate = jax.nn.sigmoid(dense(normed_cols, projections[3]))
    qcols, kcols, vcols = (split(query), split(key), split(value))
    context = join(attend_forward(qcols, kcols, vcols, bias_blocks, keep))
    gated = (gate * context.astype(jnp.float32)).astype(jnp.bfloat16)
    attended_cols = dense(gated, projections[4]).astype(jnp.bfloat16)
    attended = lax.all_to_all(attended_cols, "row", split_axis=0, concat_axis=1, tiled=True)
    d_gated = dense(cot_cols, projections[4].T)
    d_context_cols = (d_gated * gate).astype(jnp.bfloat16)
    d_gate_pre = (d_gated * context.astype(jnp.float32) * gate * (1.0 - gate)).astype(jnp.bfloat16)
    dq, dk, dv, total = attend_backward(
        qcols, kcols, vcols, split(d_context_cols), bias_blocks, keep
    )
    dq, dk, dv = (join(dq), join(dk), join(dv))
    grid = total.transpose(1, 0, 2, 3).reshape(heads, n_col, tile_cols, n_row, tile_rows)
    grid = jnp.transpose(grid, (3, 1, 0, 4, 2))
    flat = grid.reshape(n_row * n_col, heads, tile_rows, tile_cols)
    d_bias = lax.psum_scatter(flat, ("row", "col"), scatter_dimension=0, tiled=True)[0].astype(
        jnp.bfloat16
    )
    bias_term = jnp.einsum("hab,ch->abc", d_bias, bias_weight, preferred_element_type=jnp.float32)
    bias_weight_part = jnp.einsum(
        "abc,hab->ch", normalized_pair, d_bias, preferred_element_type=jnp.float32
    )
    d_cols = dense(dq, projections[0].T) + dense(dk, projections[1].T) + dense(dv, projections[2].T)
    d_cols = d_cols + dense(d_gate_pre, projections[3].T)
    parts = jnp.stack(
        [
            outer_sum(normed_cols, dq),
            outer_sum(normed_cols, dk),
            outer_sum(normed_cols, dv),
            outer_sum(normed_cols, d_gate_pre),
            outer_sum(gated, cot_cols),
        ]
    )
    normalized_gradient = (
        lax.all_to_all(d_cols, "row", split_axis=0, concat_axis=1, tiled=True) + bias_term
    )
    gain_partial_sum = jnp.sum(normalized_gradient * centered_scaled, axis=(0, 1))
    projection_grad, bias_weight_grad, gain_gradient = lax.psum(
        (parts, bias_weight_part, gain_partial_sum), ("row", "col")
    )
    scaled_output = normalized_gradient * gain
    pair_gradient = inverse_deviation * (
        scaled_output
        - jnp.mean(scaled_output, axis=-1, keepdims=True)
        - centered_scaled * jnp.mean(scaled_output * centered_scaled, axis=-1, keepdims=True)
    )
    return (attended, pair_gradient, projection_grad, bias_weight_grad, gain_gradient)


def solution(mesh):
    placed = (P("row", "col", None), P(), P(), P(), P(), P("row", "col", None))
    return jax.shard_map(
        shards,
        mesh=mesh,
        in_specs=placed,
        out_specs=(P("row", "col", None), P("row", "col", None), P(), P(), P()),
        check_vma=False,
    )
```

profile of v0, /device:TPU:8, one launch (start us, length us, event | category | flops | bytes accessed | tf_op | source)
XLA Modules:
  0.0 754.6 jit_solution(17553295921628759125)
XLA Ops:
  14.7 6.3 all-to-all-start
  24.3 25.6 %all-to-all-done = bf16[24,192,128]{2,0,1:T(8,128)(2,1)S(1)} async-done(((bf16[24,192,128]{2,0,1:T(8,128)(2,1)}), bf16[24,192,128]{2,0,1:T(8,128)(2,1)S(1)}, u32[]{:S(2)}, u32[]{:S(2)}) %all-to-all-start) | async-done | bytes 1179680 | tf_op jit(solution)/shard_map/all_to_all | solution.py:137
  49.9 5.8 all-to-all-start.2
  56.0 38.6 %all-to-all-done.2 = bf16[24,192,128]{2,0,1:T(8,128)(2,1)S(1)} async-done(((bf16[24,192,128]{2,0,1:T(8,128)(2,1)}), bf16[24,192,128]{2,0,1:T(8,128)(2,1)S(1)}, u32[]{:S(2)}, u32[]{:S(2)}) %all-to-all-start.2) | async-done | bytes 1179680 | tf_op jit(solution)/shard_map/all_to_all | solution.py:138
  102.0 6.0 copy.150
  113.1 113.0 %while.28 = (s32[]{:T(128)}, bf16[12,384,4,32]{1,3,2,0:T(8,128)(2,1)}, bf16[12,384,4,32]{1,3,2,0:T(8,128)(2,1)}, bf16[12,384,4,32]{1,3,2,0:T(8,128)(2,1)}, bf16[...) while((s32[]{:T(128)}, ...), condition=%wide.region_5.6_spmd.clone, body=%wide.region_2.5_spmd.clone.sunk | while | flops 119786112 | bytes 12402905 | solution.py:45
  226.1 4.9 fusion.92
  234.2 6.4 all-to-all-start.1
  244.1 230.7 %while.29 = (s32[]{:T(128)}, f32[1,4,384,384]{2,3,1,0:T(8,128)}, bf16[12,384,4,32]{1,3,2,0:T(8,128)(2,1)}, bf16[12,384,4,32]{1,3,2,0:T(8,128)(2,1)}, bf16[12,384...) while((s32[]{:T(128)}, f32[1,4,384,384]{2,3,1,0:T(8,128)}, ...), condition=%wide.region_10.11_spmd.clone, body=%wide.region_6.10_spmd.clone.sunk | while | flops 240305280 | bytes 59063672 | solution.py:98
  273.6 4.5 bitcast_add_fusion.4
  292.9 4.5 bitcast_add_fusion.4
  312.2 4.5 bitcast_add_fusion.4
  331.5 4.5 bitcast_add_fusion.4
  350.7 4.5 bitcast_add_fusion.4
  370.0 4.5 bitcast_add_fusion.4
  389.3 4.5 bitcast_add_fusion.4
  408.6 4.5 bitcast_add_fusion.4
  427.9 4.5 bitcast_add_fusion.4
  447.2 4.5 bitcast_add_fusion.4
  488.9 6.2 all-to-all-start.3
  513.3 99.0 %reduce-scatter.2.cloned.1.call-done = f32[1,4,24,192]{3,2,1,0:T(8,128)} async-done(((f32[32,4,24,192]{3,2,1,0:T(8,128)}), f32[1,4,24,192]{3,2,1,0:T(8,128)}) %reduce-scatter.2.cloned.1.call-update) | async-done | bytes 73744 | tf_op jit(solution)/shard_map/reduce_scatter | solution.py:159
  620.3 4.8 fusion.84
  625.1 39.1 %all-reduce = (f32[128,4]{0,1:T(4,128)}, f32[128]{0:T(128)}) all-reduce(f32[128,4]{0,1:T(4,128)S(1)} %convolution_bitcast_fusion.3, f32[128]{0:T(128)S(1)} %get-tuple-element.237), channel_id=1, replica_groups=mesh['row'=16,'col'=2] {'row','col'}, use_global_device_ids=true, to_apply=%region_15.16 | all-reduce | flops 640 | bytes 5120 | tf_op jit(solution)/shard_map/psum | solution.py:181
  664.1 82.2 %all-reduce.3.cloned.1.call-done = f32[5,128,128]{2,1,0:T(8,128)} async-done(((f32[5,128,128]{2,1,0:T(8,128)}), f32[5,128,128]{2,1,0:T(8,128)}) %all-reduce.3.cloned.1.call-update) | async-done | bytes 327696 | tf_op jit(solution)/shard_map/psum | solution.py:181
  (339 shorter events, 370.2 us)
Async XLA Ops:
  7.2 13.9 %copy-start = (bf16[128,4]{0,1:T(4,128)(2,1)S(1)}, bf16[128,4]{0,1:T(4,128)(2,1)}, u32[]{:S(2)}) copy-start(bf16[128,4]{0,1:T(4,128)(2,1)} %param.13) | copy-start | bytes 3076
  7.2 4.3 copy-start.29
  12.9 8.1 %copy-start.5 = (bf16[24,192,128]{2,1,0:T(8,128)(2,1)}, bf16[24,192,128]{2,1,0:T(8,128)(2,1)S(1)}, u32[]{:S(2)}) copy-start(bf16[24,192,128]{2,1,0:T(8,128)(2,1)S(1)} %fusion.81) | copy-start | bytes 3538948
  14.7 35.2 %all-to-all-start = ((bf16[24,192,128]{2,0,1:T(8,128)(2,1)}), bf16[24,192,128]{2,0,1:T(8,128)(2,1)S(1)}, u32[]{:S(2)}, u32[]{:S(2)}) async-start(bf16[24,192,128]{2,0,1:T(8,128)(2,1)} %copy.143), calls=%async_computation | async-start | bytes 2359296 | tf_op jit(solution)/shard_map/all_to_all | solution.py:137
  21.0 81.0 %all-gather.3.cloned.1.call-start = ((), (), s32[]{:S(2)}) async-start(), calls=%async_computation.7 | async-start | bytes 3244032 | tf_op jit(solution)/shard_map/all_gather | solution.py:126
  49.9 44.7 %all-to-all-start.2 = ((bf16[24,192,128]{2,0,1:T(8,128)(2,1)}), bf16[24,192,128]{2,0,1:T(8,128)(2,1)S(1)}, u32[]{:S(2)}, u32[]{:S(2)}) async-start(bf16[24,192,128]{2,0,1:T(8,128)(2,1)} %copy.155), calls=%async_computation.2 | async-start | bytes 2359296 | tf_op jit(solution)/shard_map/all_to_all | solution.py:138
  94.8 5.3 copy-start.9
  234.2 254.7 %all-to-all-start.1 = ((bf16[384,12,128]{2,1,0:T(8,128)(2,1)}), bf16[384,12,128]{2,1,0:T(8,128)(2,1)}, u32[]{:S(2)}, u32[]{:S(2)}) async-start(bf16[384,12,128]{2,1,0:T(8,128)(2,1)} %copy.152), calls=%async_computation.1 | async-start | bytes 3145728 | tf_op jit(solution)/shard_map/all_to_all | solution.py:148
  258.8 3.8 copy-start.2
  278.1 3.8 copy-start.2
  297.4 3.8 copy-start.2
  336.0 3.8 copy-start.2
  355.2 3.8 copy-start.2
  374.5 3.8 copy-start.2
  393.8 3.8 copy-start.2
  413.1 3.8 copy-start.2
  432.4 3.8 copy-start.2
  476.5 5.0 copy-start.13
  478.6 4.1 copy-start.11
  488.9 6.2 copy-start.4
  488.9 124.7 %all-to-all-start.3 = ((f32[384,12,128]{2,1,0:T(8,128)}), f32[384,12,128]{2,1,0:T(8,128)}, u32[]{:S(2)}, u32[]{:S(2)}) async-start(f32[384,12,128]{2,1,0:T(8,128)} %copy.165), calls=%async_computation.3 | async-start | bytes 6291456 | tf_op jit(solution)/shard_map/all_to_all | solution.py:178
  495.0 117.3 %reduce-scatter.2.cloned.1.call-start = ((), (), s32[]{:S(2)}) async-start(), calls=%async_computation.5 | async-start | bytes 3244032 | tf_op jit(solution)/shard_map/reduce_scatter | solution.py:159
  502.6 243.7 %all-reduce.3.cloned.1.call-start = ((), (), s32[]{:S(2)}) async-start(), calls=%async_computation.6 | async-start | bytes 655360 | tf_op jit(solution)/shard_map/psum | solution.py:181
  512.0 101.2 %copy-start.6 = (bf16[24,192,128]{2,1,0:T(8,128)(2,1)S(1)}, bf16[24,192,128]{2,1,0:T(8,128)(2,1)}, u32[]{:S(2)}) copy-start(bf16[24,192,128]{2,1,0:T(8,128)(2,1)} %copy-done.5) | copy-start | bytes 3538948
  (58 other events, 94.1 us)
Sparse Core Ops, SparseCore 0:
  25.3 71.1 all-gather.2
  502.7 109.5 reduce-scatter.1
  618.2 128.0 all-reduce.2
where the time goes:
time: 758 us; the launch traced here: 755 us
  matrix products  275 us (36%)
  waiting for transfers between devices  245 us (32%)
  other arithmetic  84.5 us (11%)
  local copies, waits for them, and re-layouts  71.3 us (9%)
  blocking collectives  39.1 us (5%)
  starting transfers between devices  25 us (3%)
  between operations  14.1 us (2%)
    reduce_scatter x1, waiting for transfers between devices, shards(): lax.psum_scatter(flat, ('row', 'col'), scatter_dimension=0, tiled=True)[0]  99 us
    psum x1, waiting for transfers between devices, shards(): lax.psum((parts, bias_weight_part, gain_partial_sum), ('row', 'col'))  82.2 us
    sub x24, matrix products, per_block(): probs = jax.nn.softmax(scores, axis=-1)  58.6 us
    add x12, other arithmetic, per_column(): total + dscores  53.3 us
    dot_general x12, matrix products, per_block(): jnp.einsum('hqk,qhd->khd', weights_b, dblk, preferred_element_type=jnp.fl...  45.7 us
    dot_general x12, matrix products, per_block(): jnp.einsum('hqk,khd->qhd', probs.astype(jnp.bfloat16), vcol, preferred_el...  44 us
    psum x1, blocking collectives, shards(): lax.psum((parts, bias_weight_part, gain_partial_sum), ('row', 'col'))  39.1 us
    all_to_all x1, waiting for transfers between devices, shards(): lax.all_to_all(out_cotangent, 'row', split_axis=1, concat_axis=0, tiled=T...  38.6 us
  transfers between devices with their start and end apart: 7, of which 4 were waited for; matrix products, arithmetic and copies ran while one was open for 35% of the time, Pallas kernels for 0%

commit v1 on v0

v1 whole, which is shorter than its diff:
```python
import functools

import jax
import jax.numpy as jnp
from jax import lax
from jax.experimental import pallas as pl
from jax.experimental.pallas import tpu as pltpu
from jax.sharding import PartitionSpec as P

EPS = 1e-05
F32 = jnp.float32
BF16 = jnp.bfloat16


def mm(left, right):
    return lax.dot_general(left, right, (((1,), (0,)), ((), ())), preferred_element_type=F32)


def mm_nt(left, right):
    return lax.dot_general(left, right, (((1,), (1,)), ((), ())), preferred_element_type=F32)


def attention_kernel(
    heads, valid_ref, x_ref, cot_ref, w_in_ref, w_out_ref, bias_ref,
    att_ref, dn_ref, dbias_ref, parts_ref, bias_s, dbias_s,
):
    step = pl.program_id(0)
    n_row, _, tile_rows, channels = x_ref.shape
    n_col, tile_cols = bias_ref.shape[1], bias_ref.shape[4]
    rows = n_row * tile_rows
    width = channels // heads
    scale = width ** (-0.5)
    keep_lanes = lax.broadcasted_iota(jnp.int32, (rows, 1), 0) < valid_ref[0]

    @pl.when(step == 0)
    def _():
        for h in range(heads):
            for c in range(n_col):
                block = bias_ref[:, c, h].reshape(rows, tile_cols)
                bias_s[h, :, c * tile_cols : (c + 1) * tile_cols] = jnp.where(
                    keep_lanes, block, -1000000000.0
                )
        dbias_s[...] = jnp.zeros_like(dbias_s)
        parts_ref[...] = jnp.zeros_like(parts_ref)

    x = x_ref[:, 0].astype(F32).reshape(rows, channels).astype(BF16)
    cot = cot_ref[:, 0].astype(F32).reshape(rows, channels).astype(BF16)
    proj = mm(x, w_in_ref[...])
    query = proj[:, :channels].astype(BF16)
    key_f = jnp.where(keep_lanes, proj[:, channels : 2 * channels], 0.0)
    key = key_f.astype(BF16)
    value_f = proj[:, 2 * channels : 3 * channels]
    value = value_f.astype(BF16)
    gate = jax.nn.sigmoid(proj[:, 3 * channels :])
    d_gated = mm_nt(cot, w_out_ref[...])
    d_context_f = d_gated * gate
    d_context = d_context_f.astype(BF16)
    key_t = jnp.transpose(key_f).astype(BF16)
    value_t = jnp.transpose(value_f).astype(BF16)
    lane_head = lax.broadcasted_iota(jnp.int32, (rows, channels), 1) // width
    ctx_parts, dq_parts = [], []
    dk = jnp.zeros((rows, channels), F32)
    dv = jnp.zeros((rows, channels), F32)
    for h in range(heads):
        mine = lane_head == h
        q_h = jnp.where(mine, query, jnp.zeros_like(query))
        dc_h = jnp.where(mine, d_context, jnp.zeros_like(d_context))
        s = mm_nt(key, q_h) * scale + bias_s[h]
        e = jnp.exp(s - jnp.max(s, axis=0, keepdims=True))
        p = e * (1.0 / jnp.sum(e, axis=0, keepdims=True))
        d_p = mm_nt(value, dc_h)
        delta = jnp.sum(p * d_p, axis=0, keepdims=True)
        ds = p * (d_p - delta)
        dbias_s[h] += ds
        p_b = p.astype(BF16)
        ds_b = ds.astype(BF16)
        ctx_parts.append(mm(value_t[h * width : (h + 1) * width], p_b))
        dq_parts.append(mm(key_t[h * width : (h + 1) * width], ds_b))
        dv += mm(p_b, dc_h)
        dk += mm(ds_b, q_h)
    context = jnp.transpose(jnp.concatenate(ctx_parts, axis=0)).astype(BF16).astype(F32)
    dq = (jnp.transpose(jnp.concatenate(dq_parts, axis=0)) * scale).astype(BF16)
    dk = (dk * scale).astype(BF16)
    dv = dv.astype(BF16)
    gated_f = gate * context
    gated = gated_f.astype(BF16)
    att = mm(gated, w_out_ref[...])
    att_ref[:, 0] = att.reshape(n_row, tile_rows, channels).astype(att_ref.dtype)
    d_gate = (d_gated * context * gate * (1.0 - gate)).astype(BF16)
    grads = jnp.concatenate([dq, dk, dv, d_gate], axis=1)
    dn = mm_nt(grads, w_in_ref[...])
    dn_ref[:, 0] = dn.reshape(n_row, tile_rows, channels).astype(dn_ref.dtype)
    x_t = jnp.transpose(x.astype(F32)).astype(BF16)
    parts_ref[:, : 4 * channels] += mm(x_t, grads)
    gated_t = jnp.transpose(gated.astype(F32)).astype(BF16)
    parts_ref[:, 4 * channels :] += mm(gated_t, cot)

    @pl.when(step == pl.num_programs(0) - 1)
    def _():
        for h in range(heads):
            for c in range(n_col):
                block = dbias_s[h, :, c * tile_cols : (c + 1) * tile_cols]
                dbias_ref[:, c, h] = block.reshape(n_row, tile_rows, tile_cols)


def attention(valid_len, x_cols, cot_cols, w_in, w_out, bias):
    n_row, ncols, tile_rows, channels = x_cols.shape
    heads, n_col, tile_cols = bias.shape[2], bias.shape[1], bias.shape[4]
    rows = n_row * tile_rows
    column = pl.BlockSpec((n_row, 1, tile_rows, channels), lambda j: (0, j, 0, 0))

    def whole(shape):
        return pl.BlockSpec(shape, lambda j: (0,) * len(shape))

    return pl.pallas_call(
        functools.partial(attention_kernel, heads),
        grid=(ncols,),
        in_specs=[
            pl.BlockSpec(memory_space=pltpu.SMEM),
            column,
            column,
            whole(w_in.shape),
            whole(w_out.shape),
            whole(bias.shape),
        ],
        out_specs=[column, column, whole(bias.shape), whole((channels, 5 * channels))],
        out_shape=[
            jax.ShapeDtypeStruct(x_cols.shape, BF16),
            jax.ShapeDtypeStruct(x_cols.shape, BF16),
            jax.ShapeDtypeStruct(bias.shape, F32),
            jax.ShapeDtypeStruct((channels, 5 * channels), F32),
        ],
        scratch_shapes=[
            pltpu.VMEM((heads, rows, rows), F32),
            pltpu.VMEM((heads, rows, rows), F32),
        ],
        compiler_params=pltpu.CompilerParams(
            dimension_semantics=("arbitrary",), vmem_limit_bytes=60 * 1024 * 1024
        ),
    )(valid_len, x_cols, cot_cols, w_in, w_out, bias)


def shards(pair, gain, projections, bias_weight, valid_len, out_cotangent):
    n_row = lax.axis_size("row")
    n_col = lax.axis_size("col")
    tile_rows, tile_cols, channels = pair.shape
    heads = bias_weight.shape[1]
    ncols = tile_cols // n_row
    pair_float = pair.astype(F32)
    average_value = jnp.mean(pair_float, axis=-1, keepdims=True)
    var = jnp.mean((pair_float - average_value) ** 2, axis=-1, keepdims=True)
    inverse_deviation = lax.rsqrt(var + EPS)
    centered_scaled = (pair_float - average_value) * inverse_deviation
    normalized_pair = (centered_scaled * gain).astype(BF16)
    bias_tile = jnp.einsum("abc,ch->hab", normalized_pair, bias_weight, preferred_element_type=F32)
    gathered = lax.all_gather(bias_tile[None], ("row", "col"), axis=0, tiled=True)
    gathered = gathered.reshape(n_row, n_col, heads, tile_rows, tile_cols)

    def to_columns(tile):
        moved = jnp.swapaxes(tile, 0, 1).reshape(n_row, ncols, tile_rows, channels)
        return lax.all_to_all(moved, "row", split_axis=0, concat_axis=0, tiled=True)

    def to_tile(columns):
        moved = lax.all_to_all(columns, "row", split_axis=0, concat_axis=0, tiled=True)
        return jnp.swapaxes(moved.reshape(tile_cols, tile_rows, channels), 0, 1)

    x_cols, cot_cols = to_columns(normalized_pair), to_columns(out_cotangent)
    w_in = jnp.swapaxes(projections[:4], 0, 1).reshape(channels, 4 * channels)
    att_cols, dn_cols, total, parts = attention(
        valid_len, x_cols, cot_cols, w_in, projections[4], gathered
    )
    flat = total.reshape(n_row * n_col, heads, tile_rows, tile_cols)
    d_bias = lax.psum_scatter(flat, ("row", "col"), scatter_dimension=0, tiled=True)[0].astype(BF16)
    parts = lax.psum(parts, ("row", "col"))
    projection_grad = jnp.swapaxes(parts.reshape(channels, 5, channels), 0, 1)
    attended = to_tile(att_cols)
    bias_term = jnp.einsum("hab,ch->abc", d_bias, bias_weight, preferred_element_type=F32)
    bias_weight_part = jnp.einsum(
        "abc,hab->ch", normalized_pair, d_bias, preferred_element_type=F32
    )
    normalized_gradient = to_tile(dn_cols).astype(F32) + bias_term
    gain_partial_sum = jnp.sum(normalized_gradient * centered_scaled, axis=(0, 1))
    bias_weight_grad, gain_gradient = lax.psum((bias_weight_part, gain_partial_sum), ("row", "col"))
    scaled_output = normalized_gradient * gain
    pair_gradient = inverse_deviation * (
        scaled_output
        - jnp.mean(scaled_output, axis=-1, keepdims=True)
        - centered_scaled * jnp.mean(scaled_output * centered_scaled, axis=-1, keepdims=True)
    )
    return (attended, pair_gradient, projection_grad, bias_weight_grad, gain_gradient)


def solution(mesh):
    placed = (P("row", "col", None), P(), P(), P(), P(), P("row", "col", None))
    return jax.shard_map(
        shards,
        mesh=mesh,
        in_specs=placed,
        out_specs=(P("row", "col", None), P("row", "col", None), P(), P(), P()),
        check_vma=False,
    )
```

time: 758 us -> 468 us (0.62)
  matrix products: 275 us -> 9.27 us
  other arithmetic: 84.5 us -> 15.4 us
  local copies, waits for them, and re-layouts: 71.3 us -> 12.3 us
  waiting for transfers between devices: 245 us -> 302 us
  Pallas kernels: 0 us -> 47.1 us
    dot_general x88 -> x1, matrix products: 215 us -> 4.56 us  [shards(): jnp.einsum('hab,ch->abc', d_bias, bias_weight, preferred_element_type=F32)]
    sub x24 -> x0, matrix products: 58.6 us -> none  [per_block(): probs = jax.nn.softmax(scores, axis=-1)]
    add x12 -> x0, other arithmetic: 53.3 us -> none  [per_column(): total + dscores]
    pallas_call x0 -> x1, Pallas kernels: none -> 47.1 us  [attention(): pl.pallas_call(functools.partial(attention_kernel, heads), grid=(ncols,),...]
    psum x1, waiting for transfers between devices: 82.2 us -> 114 us  [shards(): parts = lax.psum(parts, ('row', 'col'))]
    all_to_all x4, waiting for transfers between devices: 64.2 us -> 85.6 us  [the longest x2 59.5 us: to_columns(): return lax.all_to_all(moved, 'row', split_axis=0, concat_axis=0, tiled=True)]
    while x96 -> x0, local copies, waits for them, and re-layouts: 20.8 us -> none
    another operation x7 -> x0, local copies, waits for them, and re-layouts: 16 us -> none  [the longest x2 7.47 us: shards(): total.transpose(1, 0, 2, 3)]
  transfers between devices with their start and end apart: 7 -> 7, of which waited for: 4 -> 5; matrix products, arithmetic and copies ran while one was open for 35% -> 3% of each run, Pallas kernels for 0% -> 0%
where the time goes in v1:
time: 468 us; the launch traced here: 464 us
  waiting for transfers between devices  302 us (65%)
  Pallas kernels  47.1 us (10%)
  blocking collectives  39.1 us (8%)
  starting transfers between devices  24.6 us (5%)
  other arithmetic  15.4 us (3%)
  between operations  14.6 us (3%)
  local copies, waits for them, and re-layouts  12.3 us (3%)
  matrix products  9.27 us (2%)
    psum x1, waiting for transfers between devices, shards(): parts = lax.psum(parts, ('row', 'col'))  114 us
    reduce_scatter x1, waiting for transfers between devices, shards(): lax.psum_scatter(flat, ('row', 'col'), scatter_dimension=0, tiled=True)[0]  102 us
    all_to_all x2, waiting for transfers between devices, to_columns(): return lax.all_to_all(moved, 'row', split_axis=0, concat_axis=0, tiled=True)  59.5 us
    pallas_call x1, Pallas kernels, attention(): pl.pallas_call(functools.partial(attention_kernel, heads), grid=(ncols,),...  47.1 us
    psum x1, blocking collectives, shards(): lax.psum((bias_weight_part, gain_partial_sum), ('row', 'col'))  39.1 us
    all_to_all x2, waiting for transfers between devices, to_tile(): lax.all_to_all(columns, 'row', split_axis=0, concat_axis=0, tiled=True)  26 us
    all_to_all x2, starting transfers between devices, to_columns(): return lax.all_to_all(moved, 'row', split_axis=0, concat_axis=0, tiled=True)  13 us
    all_to_all x2, starting transfers between devices, to_tile(): lax.all_to_all(columns, 'row', split_axis=0, concat_axis=0, tiled=True)  11.5 us
  transfers between devices with their start and end apart: 7, of which 5 were waited for; matrix products, arithmetic and copies ran while one was open for 3% of the time, Pallas kernels for 0%

profile of v1, /device:TPU:8, one launch (start us, length us, event | category | flops | bytes accessed | tf_op | source)
XLA Modules:
  0.0 464.2 jit_solution(9163946209713172294)
XLA Ops:
  7.2 1.9 convert_reduce_fusion
  9.1 2.8 fusion.11
  12.0 2.0 convolution_bitcast_fusion
  14.6 1.5 fusion.14
  16.1 1.8 copy.28
  17.9 6.3 %all-to-all-start = ((bf16[16,12,24,128]{3,2,1,0:T(8,128)(2,1)}), bf16[16,12,24,128]{3,2,1,0:T(8,128)(2,1)S(1)}, u32[]{:S(2)}, u32[]{:S(2)}) async-start(bf16[16,12,24,128]{3,2,1,0:T(8,128)(2,1)} %bitcast.1), calls=%async_computation | async-start | bytes 2359296 | tf_op jit(solution)/shard_map/all_to_all | solution.py:161
  24.2 1.8 copy.29
  26.0 27.5 %all-to-all-done.x_ref = bf16[16,12,24,128]{3,2,1,0:T(8,128)(2,1)S(1)} async-done(((bf16[16,12,24,128]{3,2,1,0:T(8,128)(2,1)}), bf16[16,12,24,128]{3,2,1,0:T(8,128)(2,1)S(1)}, u32[]{:S(2)}, u32[]{:S(2)}) %all-to-all-start) | async-done | bytes 1179680 | tf_op jit(solution)/shard_map/all_to_all | solution.py:161
  53.5 6.7 %all-to-all-start.1 = ((bf16[16,12,24,128]{3,2,1,0:T(8,128)(2,1)}), bf16[16,12,24,128]{3,2,1,0:T(8,128)(2,1)S(1)}, u32[]{:S(2)}, u32[]{:S(2)}) async-start(bf16[16,12,24,128]{3,2,1,0:T(8,128)(2,1)} %bitcast.3), calls=%async_computation.1 | async-start | bytes 2359296 | tf_op jit(solution)/shard_map/all_to_all | solution.py:161
  60.9 1.4 slice_bitcast_fusion.1.w_out_ref
  62.2 1.6 copy_bitcast_fusion.1.w_in_ref
  63.8 32.0 %all-to-all-done.1.cot_ref = bf16[16,12,24,128]{3,2,1,0:T(8,128)(2,1)S(1)} async-done(((bf16[16,12,24,128]{3,2,1,0:T(8,128)(2,1)}), bf16[16,12,24,128]{3,2,1,0:T(8,128)(2,1)S(1)}, u32[]{:S(2)}, u32[]{:S(2)}) %all-to-all-start.1) | async-done | bytes 1179680 | tf_op jit(solution)/shard_map/all_to_all | solution.py:161
  96.8 47.1 %shard_map.101 = (bf16[16,12,24,128]{3,2,1,0:T(8,128)(2,1)}, bf16[16,12,24,128]{3,2,1,0:T(8,128)(2,1)}, f32[16,2,4,24,192]{4,3,2,1,0:T(8,128)}, f32[128,640]{1,0:T(8,128)}) custom-call(s32[1]{0:T(128)S(6)} %copy.50.valid_ref, bf16[16,12,24,128]{3,2,1,0:T(8,128)(2,1)} %copy-done.2, bf16[16,12,24,128]{3,2,1,0:T(8,128)(2,1)} %copy-done.3, ...), custom_call_target="tpu_custom_call" | custom-call | tf_op jit(solution)/shard_map/pallas_call | solution.py:115
  144.0 5.9 %all-to-all-start.2 = ((bf16[16,12,24,128]{3,2,1,0:T(8,128)(2,1)}), bf16[16,12,24,128]{3,2,1,0:T(8,128)(2,1)S(1)}, u32[]{:S(2)}, u32[]{:S(2)}) async-start(bf16[16,12,24,128]{3,2,1,0:T(8,128)(2,1)} %get-tuple-element.9), calls=%async_computation.2 | async-start | bytes 2359296 | tf_op jit(solution)/shard_map/all_to_all | solution.py:164
  151.6 26.0 %all-to-all-done.2 = bf16[16,12,24,128]{3,2,1,0:T(8,128)(2,1)S(1)} async-done(((bf16[16,12,24,128]{3,2,1,0:T(8,128)(2,1)}), bf16[16,12,24,128]{3,2,1,0:T(8,128)(2,1)S(1)}, u32[]{:S(2)}, u32[]{:S(2)}) %all-to-all-start.2) | async-done | bytes 1179680 | tf_op jit(solution)/shard_map/all_to_all | solution.py:164
  177.7 5.6 %all-to-all-start.3 = ((bf16[16,12,24,128]{3,2,1,0:T(8,128)(2,1)}), bf16[16,12,24,128]{3,2,1,0:T(8,128)(2,1)S(1)}, u32[]{:S(2)}, u32[]{:S(2)}) async-start(bf16[16,12,24,128]{3,2,1,0:T(8,128)(2,1)} %get-tuple-element.10), calls=%async_computation.3 | async-start | bytes 2359296 | tf_op jit(solution)/shard_map/all_to_all | solution.py:164
  183.2 113.7 %all-reduce.3.cloned.1.call-done = f32[5,128,128]{1,2,0:T(8,128)} async-done(((f32[5,128,128]{1,2,0:T(8,128)}), f32[5,128,128]{1,2,0:T(8,128)}) %all-reduce.3.cloned.1.call-update) | async-done | bytes 327696 | tf_op jit(solution)/shard_map/psum | solution.py:174
  297.0 1.9 copy.37
  300.1 1.6 bitcast_convert_fusion
  301.8 101.8 %reduce-scatter.2.cloned.1.call-done = f32[1,4,24,192]{3,2,1,0:T(8,128)} async-done(((f32[32,4,24,192]{3,2,1,0:T(8,128)}), f32[1,4,24,192]{3,2,1,0:T(8,128)}) %reduce-scatter.2.cloned.1.call-update) | async-done | bytes 73744 | tf_op jit(solution)/shard_map/reduce_scatter | solution.py:173
  404.6 2.7 convolution_bitcast_fusion.1
  407.4 4.6 fusion.10
  411.9 39.1 %all-reduce = (f32[128,4]{0,1:T(4,128)}, f32[128]{0:T(128)}) all-reduce(f32[128,4]{0,1:T(4,128)S(1)} %convolution_bitcast_fusion.1, f32[128]{0:T(128)S(1)} %get-tuple-element.23), channel_id=1, replica_groups=mesh['row'=16,'col'=2] {'row','col'}, use_global_device_ids=true, to_apply=%region_6.0 | all-reduce | flops 640 | bytes 5120 | tf_op jit(solution)/shard_map/psum | solution.py:183
  451.8 5.9 %fusion.9 = f32[24,192,128]{2,1,0:T(8,128)} fusion(bf16[24,192,128]{2,1,0:T(8,128)(2,1)S(1)} %copy-done.1, f32[24,192,128]{2,1,0:T(8,128)S(1)} %get-tuple-element.28, f32[24,192]{1,0:T(8,128)S(1)} %get-tuple-element.29, f32[24,192]{1,0:T(8,128)S(1)} %get-tuple-element.30, f32[128]{0:T(128)S(1)} %copy-done.13, f32[24,192]{1,0:T(8,128)} %copy-done.10, ...), kind=kLoop, calls=%fused_computation.11 | loop fusion | flops 4718592 | bytes 5972480 | tf_op jit(solution)/shard_map/mul | solution.py:185
  (43 shorter events, 6.6 us)
Async XLA Ops:
  7.2 4.8 %copy-start = (bf16[128,4]{0,1:T(4,128)(2,1)S(1)}, bf16[128,4]{0,1:T(4,128)(2,1)}, u32[]{:S(2)}) copy-start(bf16[128,4]{0,1:T(4,128)(2,1)} %param.9) | copy-start | bytes 3076
  7.2 4.8 %copy-start.1 = (bf16[24,192,128]{2,1,0:T(8,128)(2,1)S(1)}, bf16[24,192,128]{2,1,0:T(8,128)(2,1)}, u32[]{:S(2)}) copy-start(bf16[24,192,128]{2,1,0:T(8,128)(2,1)} %param.6) | copy-start | bytes 3538948
  7.2 4.8 %copy-start.13 = (f32[128]{0:T(128)S(1)}, f32[128]{0:T(128)}, u32[]{:S(2)}) copy-start(f32[128]{0:T(128)} %param.7) | copy-start | bytes 1540
  7.2 88.6 %all-gather.3.cloned.1.call-start = ((), (), s32[]{:S(2)}) async-start(), calls=%async_computation.7 | async-start | bytes 3244032 | tf_op jit(solution)/shard_map/all_gather | solution.py:156
  9.1 8.8 %copy-start.6 = (f32[24,192]{1,0:T(8,128)}, f32[24,192]{1,0:T(8,128)S(1)}, u32[]{:S(2)}) copy-start(f32[24,192]{1,0:T(8,128)S(1)} %broadcast_multiply_fusion.2) | copy-start | bytes 55300
  12.0 4.1 copy-start.10
  16.1 8.1 %copy-start.5 = (bf16[24,192,128]{2,1,0:T(8,128)(2,1)S(1)}, bf16[24,192,128]{2,1,0:T(8,128)(2,1)}, u32[]{:S(2)}) copy-start(bf16[24,192,128]{2,1,0:T(8,128)(2,1)} %param.11) | copy-start | bytes 3538948
  17.9 35.6 %all-to-all-start = ((bf16[16,12,24,128]{3,2,1,0:T(8,128)(2,1)}), bf16[16,12,24,128]{3,2,1,0:T(8,128)(2,1)S(1)}, u32[]{:S(2)}, u32[]{:S(2)}) async-start(bf16[16,12,24,128]{3,2,1,0:T(8,128)(2,1)} %bitcast.1), calls=%async_computation | async-start | bytes 2359296 | tf_op jit(solution)/shard_map/all_to_all | solution.py:161
  53.5 42.3 %copy-start.2 = (bf16[16,12,24,128]{3,2,1,0:T(8,128)(2,1)}, bf16[16,12,24,128]{3,2,1,0:T(8,128)(2,1)S(1)}, u32[]{:S(2)}) copy-start(bf16[16,12,24,128]{3,2,1,0:T(8,128)(2,1)S(1)} %all-to-all-done.x_ref) | copy-start | bytes 3538948
  53.5 42.3 %all-to-all-start.1 = ((bf16[16,12,24,128]{3,2,1,0:T(8,128)(2,1)}), bf16[16,12,24,128]{3,2,1,0:T(8,128)(2,1)S(1)}, u32[]{:S(2)}, u32[]{:S(2)}) async-start(bf16[16,12,24,128]{3,2,1,0:T(8,128)(2,1)} %bitcast.3), calls=%async_computation.1 | async-start | bytes 2359296 | tf_op jit(solution)/shard_map/all_to_all | solution.py:161
  95.8 1.0 copy-start.3
  144.0 6.0 %copy-start.9 = (f32[128,640]{1,0:T(8,128)S(1)}, f32[128,640]{1,0:T(8,128)}, u32[]{:S(2)}) copy-start(f32[128,640]{1,0:T(8,128)} %get-tuple-element.12) | copy-start | bytes 983044
  144.0 33.7 %all-to-all-start.2 = ((bf16[16,12,24,128]{3,2,1,0:T(8,128)(2,1)}), bf16[16,12,24,128]{3,2,1,0:T(8,128)(2,1)S(1)}, u32[]{:S(2)}, u32[]{:S(2)}) async-start(bf16[16,12,24,128]{3,2,1,0:T(8,128)(2,1)} %get-tuple-element.9), calls=%async_computation.2 | async-start | bytes 2359296 | tf_op jit(solution)/shard_map/all_to_all | solution.py:164
  149.9 147.1 %all-reduce.3.cloned.1.call-start = ((), (), s32[]{:S(2)}) async-start(), calls=%async_computation.6 | async-start | bytes 655360 | tf_op jit(solution)/shard_map/psum | solution.py:174
  150.9 252.6 %reduce-scatter.2.cloned.1.call-start = ((), (), s32[]{:S(2)}) async-start(), calls=%async_computation.5 | async-start | bytes 3244032 | tf_op jit(solution)/shard_map/reduce_scatter | solution.py:173
  177.7 122.5 %all-to-all-start.3 = ((bf16[16,12,24,128]{3,2,1,0:T(8,128)(2,1)}), bf16[16,12,24,128]{3,2,1,0:T(8,128)(2,1)S(1)}, u32[]{:S(2)}, u32[]{:S(2)}) async-start(bf16[16,12,24,128]{3,2,1,0:T(8,128)(2,1)} %get-tuple-element.10), calls=%async_computation.3 | async-start | bytes 2359296 | tf_op jit(solution)/shard_map/all_to_all | solution.py:164
  300.1 104.5 %copy-start.7 = (f32[24,192]{1,0:T(8,128)S(1)}, f32[24,192]{1,0:T(8,128)}, u32[]{:S(2)}) copy-start(f32[24,192]{1,0:T(8,128)} %copy-done.6) | copy-start | bytes 55300
  300.1 104.5 %copy-start.11 = (f32[24,192]{1,0:T(8,128)S(1)}, f32[24,192]{1,0:T(8,128)}, u32[]{:S(2)}) copy-start(f32[24,192]{1,0:T(8,128)} %copy-done.10) | copy-start | bytes 55300
  403.5 3.8 copy-start.4
  403.5 3.8 copy-start.8
  403.5 3.8 copy-start.12
Sparse Core Ops, SparseCore 0:
  14.8 77.8 all-gather.2
  156.6 140.2 all-reduce.2
  302.4 101.0 reduce-scatter.1

commit v2 on v1

--- a/solution.py
+++ b/solution.py
@@ -100,7 +100,7 @@
         for h in range(heads):
             for c in range(n_col):
                 block = dbias_s[h, :, c * tile_cols : (c + 1) * tile_cols]
-                dbias_ref[:, c, h] = block.reshape(n_row, tile_rows, tile_cols)
+                dbias_ref[:, c, h] = block.reshape(n_row, tile_rows, tile_cols).astype(dbias_ref.dtype)
 
 
 def attention(valid_len, x_cols, cot_cols, w_in, w_out, bias):
@@ -127,7 +127,7 @@
         out_shape=[
             jax.ShapeDtypeStruct(x_cols.shape, BF16),
             jax.ShapeDtypeStruct(x_cols.shape, BF16),
-            jax.ShapeDtypeStruct(bias.shape, F32),
+            jax.ShapeDtypeStruct(bias.shape, BF16),
             jax.ShapeDtypeStruct((channels, 5 * channels), F32),
         ],
         scratch_shapes=[
@@ -169,18 +169,29 @@
     att_cols, dn_cols, total, parts = attention(
         valid_len, x_cols, cot_cols, w_in, projections[4], gathered
     )
-    flat = total.reshape(n_row * n_col, heads, tile_rows, tile_cols)
-    d_bias = lax.psum_scatter(flat, ("row", "col"), scatter_dimension=0, tiled=True)[0].astype(BF16)
-    parts = lax.psum(parts, ("row", "col"))
-    projection_grad = jnp.swapaxes(parts.reshape(channels, 5, channels), 0, 1)
+    everyone = ("row", "col")
+    n_all = n_row * n_col
+
+    def swap(blocks):
+        return lax.all_to_all(blocks, everyone, split_axis=0, concat_axis=0, tiled=True)
+
+    shares = swap(total.reshape(n_all, heads, tile_rows, tile_cols))
+    d_bias = jnp.sum(shares.astype(F32), axis=0).astype(BF16)
+    parts = jnp.swapaxes(parts.reshape(channels, 5, channels), 0, 1)
+    slab = 5 * channels // n_all
+    owned = jnp.sum(swap(parts.reshape(n_all, slab, channels)), axis=0)
     attended = to_tile(att_cols)
     bias_term = jnp.einsum("hab,ch->abc", d_bias, bias_weight, preferred_element_type=F32)
     bias_weight_part = jnp.einsum(
-        "abc,hab->ch", normalized_pair, d_bias, preferred_element_type=F32
+        "hab,abc->hc", d_bias, normalized_pair, preferred_element_type=F32
     )
     normalized_gradient = to_tile(dn_cols).astype(F32) + bias_term
     gain_partial_sum = jnp.sum(normalized_gradient * centered_scaled, axis=(0, 1))
-    bias_weight_grad, gain_gradient = lax.psum((bias_weight_part, gain_partial_sum), ("row", "col"))
+    mine = jnp.concatenate([owned, bias_weight_part, gain_partial_sum[None]], axis=0)
+    spread = swap(jnp.broadcast_to(mine[None], (n_all,) + mine.shape))
+    projection_grad = spread[:, :slab].reshape(5, channels, channels)
+    small = jnp.sum(spread[:, slab:], axis=0)
+    bias_weight_grad, gain_gradient = small[:heads].T, small[heads]
     scaled_output = normalized_gradient * gain
     pair_gradient = inverse_deviation * (
         scaled_output

time: 468 us -> 303 us (0.65)
  waiting for transfers between devices: 302 us -> 80.4 us
  blocking collectives: 39.1 us -> 90.2 us
  local copies, waits for them, and re-layouts: 12.3 us -> 17.4 us
    psum x1 -> x0, waiting for transfers between devices: 114 us -> none  [shards(): parts = lax.psum(parts, ('row', 'col'))]
    reduce_scatter x1 -> x0, waiting for transfers between devices: 102 us -> none  [shards(): lax.psum_scatter(flat, ('row', 'col'), scatter_dimension=0, tiled=True)[0]]
    all_to_all x0 -> x3, blocking collectives: none -> 90.2 us  [the longest x2 57 us: swap(): lax.all_to_all(blocks, everyone, split_axis=0, concat_axis=0, tiled=True)]
    psum x1 -> x0, blocking collectives: 39.1 us -> none  [shards(): lax.psum((bias_weight_part, gain_partial_sum), ('row', 'col'))]
    all_to_all x2 -> x1, waiting for transfers between devices: 26 us -> 15 us  [to_tile(): lax.all_to_all(columns, 'row', split_axis=0, concat_axis=0, tiled=True)]
    all_to_all x2 -> x1, starting transfers between devices: 11.5 us -> 5.54 us  [to_tile(): lax.all_to_all(columns, 'row', split_axis=0, concat_axis=0, tiled=True)]
    all_to_all x0 -> x1, starting transfers between devices: none -> 5.84 us  [swap(): lax.all_to_all(blocks, everyone, split_axis=0, concat_axis=0, tiled=True)]
    all_to_all x0 -> x1, waiting for transfers between devices: none -> 5.82 us  [swap(): lax.all_to_all(blocks, everyone, split_axis=0, concat_axis=0, tiled=True)]
  transfers between devices with their start and end apart: 7 -> 5, of which waited for: 5 -> 4; matrix products, arithmetic and copies ran while one was open for 3% -> 9% of each run, Pallas kernels for 0% -> 0%
where the time goes in v2:
time: 303 us; the launch traced here: 299 us
  blocking collectives  90.2 us (30%)
  waiting for transfers between devices  80.4 us (27%)
  Pallas kernels  46.4 us (15%)
  starting transfers between devices  24.4 us (8%)
  local copies, waits for them, and re-layouts  17.4 us (6%)
  other arithmetic  16.3 us (5%)
  between operations  15 us (5%)
  matrix products  9.42 us (3%)
    all_to_all x2, waiting for transfers between devices, to_columns(): return lax.all_to_all(moved, 'row', split_axis=0, concat_axis=0, tiled=True)  59.5 us
    all_to_all x2, blocking collectives, swap(): lax.all_to_all(blocks, everyone, split_axis=0, concat_axis=0, tiled=True)  57 us
    pallas_call x1, Pallas kernels, attention(): pl.pallas_call(functools.partial(attention_kernel, heads), grid=(ncols,),...  46.4 us
    all_to_all x1, blocking collectives, to_tile(): lax.all_to_all(columns, 'row', split_axis=0, concat_axis=0, tiled=True)  33.2 us
    all_to_all x1, waiting for transfers between devices, to_tile(): lax.all_to_all(columns, 'row', split_axis=0, concat_axis=0, tiled=True)  15 us
    all_to_all x2, starting transfers between devices, to_columns(): return lax.all_to_all(moved, 'row', split_axis=0, concat_axis=0, tiled=True)  13 us
  transfers between devices with their start and end apart: 5, of which 4 were waited for; matrix products, arithmetic and copies ran while one was open for 9% of the time, Pallas kernels for 0%

profile of v2, /device:TPU:8, one launch (start us, length us, event | category | flops | bytes accessed | tf_op | source)
XLA Modules:
  0.0 299.4 jit_solution(8153789767810938277)
XLA Ops:
  7.2 1.8 convert_reduce_fusion
  9.1 2.8 fusion.11
  12.0 2.0 convolution_bitcast_fusion
  16.1 1.8 copy.25
  17.9 6.3 %all-to-all-start = ((bf16[16,12,24,128]{3,2,1,0:T(8,128)(2,1)}), bf16[16,12,24,128]{3,2,1,0:T(8,128)(2,1)S(1)}, u32[]{:S(2)}, u32[]{:S(2)}) async-start(bf16[16,12,24,128]{3,2,1,0:T(8,128)(2,1)} %bitcast.1), calls=%async_computation | async-start | bytes 2359296 | tf_op jit(solution)/shard_map/all_to_all | solution.py:161
  24.2 1.8 copy.26
  26.0 27.5 %all-to-all-done.x_ref = bf16[16,12,24,128]{3,2,1,0:T(8,128)(2,1)S(1)} async-done(((bf16[16,12,24,128]{3,2,1,0:T(8,128)(2,1)}), bf16[16,12,24,128]{3,2,1,0:T(8,128)(2,1)S(1)}, u32[]{:S(2)}, u32[]{:S(2)}) %all-to-all-start) | async-done | bytes 1179680 | tf_op jit(solution)/shard_map/all_to_all | solution.py:161
  53.5 6.7 %all-to-all-start.1 = ((bf16[16,12,24,128]{3,2,1,0:T(8,128)(2,1)}), bf16[16,12,24,128]{3,2,1,0:T(8,128)(2,1)S(1)}, u32[]{:S(2)}, u32[]{:S(2)}) async-start(bf16[16,12,24,128]{3,2,1,0:T(8,128)(2,1)} %bitcast.3), calls=%async_computation.1 | async-start | bytes 2359296 | tf_op jit(solution)/shard_map/all_to_all | solution.py:161
  62.2 1.6 copy_bitcast_fusion.1.w_in_ref
  63.8 32.0 %all-to-all-done.1.cot_ref = bf16[16,12,24,128]{3,2,1,0:T(8,128)(2,1)S(1)} async-done(((bf16[16,12,24,128]{3,2,1,0:T(8,128)(2,1)}), bf16[16,12,24,128]{3,2,1,0:T(8,128)(2,1)S(1)}, u32[]{:S(2)}, u32[]{:S(2)}) %all-to-all-start.1) | async-done | bytes 1179680 | tf_op jit(solution)/shard_map/all_to_all | solution.py:161
  96.9 46.4 %shard_map.101 = (bf16[16,12,24,128]{3,2,1,0:T(8,128)(2,1)}, bf16[16,12,24,128]{3,2,1,0:T(8,128)(2,1)}, bf16[16,2,4,24,192]{4,3,2,1,0:T(8,128)(2,1)}, f32[128,640]{1,0:T(8,128)}) custom-call(s32[1]{0:T(128)S(6)} %copy.46.valid_ref, bf16[16,12,24,128]{3,2,1,0:T(8,128)(2,1)} %copy-done.2, bf16[16,12,24,128]{3,2,1,0:T(8,128)(2,1)} %copy-done.3, ...), custom_call_target="tpu_custom_call" | custom-call | tf_op jit(solution)/shard_map/pallas_call | solution.py:115
  144.8 16.7 %all_to_all.35 = f32[32,20,128]{2,1,0:T(8,128)S(1)} all-to-all(f32[32,20,128]{2,1,0:T(8,128)S(1)} %reshape.69), channel_id=1, replica_groups=mesh['row'=16,'col'=2] {'row','col'}, dimensions={0} | all-to-all | bytes 655360 | tf_op jit(solution)/shard_map/all_to_all | solution.py:176
  161.5 33.2 %all_to_all.36 = bf16[16,12,24,128]{3,2,1,0:T(8,128)(2,1)} all-to-all(bf16[16,12,24,128]{3,2,1,0:T(8,128)(2,1)S(1)} %copy-done.6), channel_id=1, replica_groups=mesh['row'=16,'col'=2] {'row'}, dimensions={0} | all-to-all | bytes 2359296 | tf_op jit(solution)/shard_map/all_to_all | solution.py:164
  194.7 40.3 %all_to_all.37 = bf16[32,4,24,192]{3,2,1,0:T(8,128)(2,1)S(1)} all-to-all(bf16[32,4,24,192]{3,2,1,0:T(8,128)(2,1)} %bitcast.44), channel_id=1, replica_groups=mesh['row'=16,'col'=2] {'row','col'}, dimensions={0} | all-to-all | bytes 2359296 | tf_op jit(solution)/shard_map/all_to_all | solution.py:176
  234.9 5.5 %all-to-all-start.2 = ((bf16[16,12,24,128]{3,2,1,0:T(8,128)(2,1)}), bf16[16,12,24,128]{3,2,1,0:T(8,128)(2,1)}, u32[]{:S(2)}, u32[]{:S(2)}) async-start(bf16[16,12,24,128]{3,2,1,0:T(8,128)(2,1)} %get-tuple-element.9), calls=%async_computation.2 | async-start | bytes 2359296 | tf_op jit(solution)/shard_map/all_to_all | solution.py:164
  240.5 2.8 bitcast_convert_fusion
  244.3 1.8 convolution_bitcast_fusion.1
  246.2 5.6 %fusion.10 = (f32[128]{0:T(128)S(1)}, f32[24,192]{1,0:T(8,128)}, f32[24,192]{1,0:T(8,128)}, f32[24,192,128]{2,1,0:T(8,128)S(1)}) fusion(bf16[24,192,128]{2,1,0:T(8,128)(2,1)S(1)} %copy-done.1, f32[24,192]{1,0:T(8,128)S(1)} %copy-done.13, f32[24,192]{1,0:T(8,128)S(1)} %copy-done.9, f32[128]{0:T(128)S(1)} %copy-done.20, bf16[128,4]{0,1:T(4,128)(2,1)S(1)} %copy-done, ...), kind=kOutput, calls=%fused_computation.12 | convolution fusion | flops 10607488 | bytes 6010880 | tf_op jit(solution)/shard_map/hab,ch->abc/dot_general | solution.py:184
  252.4 15.0 %all-to-all-done.2 = bf16[16,12,24,128]{3,2,1,0:T(8,128)(2,1)} async-done(((bf16[16,12,24,128]{3,2,1,0:T(8,128)(2,1)}), bf16[16,12,24,128]{3,2,1,0:T(8,128)(2,1)}, u32[]{:S(2)}, u32[]{:S(2)}) %all-to-all-start.2) | async-done | bytes 1179680 | tf_op jit(solution)/shard_map/all_to_all | solution.py:164
  267.4 1.6 broadcast_in_dim.8
  269.0 5.8 %all-to-all-start.6 = ((f32[32,25,128]{2,1,0:T(8,128)}), f32[32,25,128]{2,1,0:T(8,128)}, u32[]{:S(2)}, u32[]{:S(2)}) async-start(f32[32,25,128]{2,1,0:T(8,128)} %broadcast_in_dim.8), calls=%async_computation.6 | async-start | bytes 1048576 | tf_op jit(solution)/shard_map/all_to_all | solution.py:176
  274.9 2.6 copy.45
  277.5 5.4 %fusion.9 = f32[24,192,128]{2,1,0:T(8,128)} fusion(bf16[24,192,128]{2,1,0:T(8,128)(2,1)S(1)} %copy-done.1, f32[24,192,128]{2,1,0:T(8,128)S(1)} %get-tuple-element.16, f32[24,192]{1,0:T(8,128)S(1)} %get-tuple-element.17, f32[24,192]{1,0:T(8,128)S(1)} %get-tuple-element.18, f32[128]{0:T(128)} %param.7, f32[24,192]{1,0:T(8,128)S(1)} %copy-done.14, ...), kind=kLoop, calls=%fused_computation.11 | loop fusion | flops 4718592 | bytes 5972480 | tf_op jit(solution)/shard_map/mul | solution.py:196
  282.9 5.8 %all-to-all-done.6 = f32[32,25,128]{2,1,0:T(8,128)} async-done(((f32[32,25,128]{2,1,0:T(8,128)}), f32[32,25,128]{2,1,0:T(8,128)}, u32[]{:S(2)}, u32[]{:S(2)}) %all-to-all-start.6) | async-done | bytes 409632 | tf_op jit(solution)/shard_map/all_to_all | solution.py:176
  (62 shorter events, 11.5 us)
Async XLA Ops:
  7.2 4.8 %copy-start = (bf16[128,4]{0,1:T(4,128)(2,1)S(1)}, bf16[128,4]{0,1:T(4,128)(2,1)}, u32[]{:S(2)}) copy-start(bf16[128,4]{0,1:T(4,128)(2,1)} %param.9) | copy-start | bytes 3076
  7.2 4.8 %copy-start.1 = (bf16[24,192,128]{2,1,0:T(8,128)(2,1)S(1)}, bf16[24,192,128]{2,1,0:T(8,128)(2,1)}, u32[]{:S(2)}) copy-start(bf16[24,192,128]{2,1,0:T(8,128)(2,1)} %param.6) | copy-start | bytes 3538948
  7.2 4.8 %copy-start.18 = (f32[128]{0:T(128)S(1)}, f32[128]{0:T(128)}, u32[]{:S(2)}) copy-start(f32[128]{0:T(128)} %param.7) | copy-start | bytes 1540
  7.2 88.6 %all-gather.3.cloned.1.call-start = ((), (), s32[]{:S(2)}) async-start(), calls=%async_computation.7 | async-start | bytes 3244032 | tf_op jit(solution)/shard_map/all_gather | solution.py:156
  9.1 7.0 %copy-start.7 = (f32[24,192]{1,0:T(8,128)}, f32[24,192]{1,0:T(8,128)S(1)}, u32[]{:S(2)}) copy-start(f32[24,192]{1,0:T(8,128)S(1)} %broadcast_multiply_fusion.2) | copy-start | bytes 55300
  12.0 4.2 %copy-start.11 = (f32[24,192]{1,0:T(8,128)}, f32[24,192]{1,0:T(8,128)S(1)}, u32[]{:S(2)}) copy-start(f32[24,192]{1,0:T(8,128)S(1)} %add_rsqrt_fusion) | copy-start | bytes 55300
  16.1 8.1 %copy-start.5 = (bf16[24,192,128]{2,1,0:T(8,128)(2,1)S(1)}, bf16[24,192,128]{2,1,0:T(8,128)(2,1)}, u32[]{:S(2)}) copy-start(bf16[24,192,128]{2,1,0:T(8,128)(2,1)} %param.11) | copy-start | bytes 3538948
  17.9 35.6 %all-to-all-start = ((bf16[16,12,24,128]{3,2,1,0:T(8,128)(2,1)}), bf16[16,12,24,128]{3,2,1,0:T(8,128)(2,1)S(1)}, u32[]{:S(2)}, u32[]{:S(2)}) async-start(bf16[16,12,24,128]{3,2,1,0:T(8,128)(2,1)} %bitcast.1), calls=%async_computation | async-start | bytes 2359296 | tf_op jit(solution)/shard_map/all_to_all | solution.py:161
  53.5 42.3 %copy-start.2 = (bf16[16,12,24,128]{3,2,1,0:T(8,128)(2,1)}, bf16[16,12,24,128]{3,2,1,0:T(8,128)(2,1)S(1)}, u32[]{:S(2)}) copy-start(bf16[16,12,24,128]{3,2,1,0:T(8,128)(2,1)S(1)} %all-to-all-done.x_ref) | copy-start | bytes 3538948
  53.5 42.3 %all-to-all-start.1 = ((bf16[16,12,24,128]{3,2,1,0:T(8,128)(2,1)}), bf16[16,12,24,128]{3,2,1,0:T(8,128)(2,1)S(1)}, u32[]{:S(2)}, u32[]{:S(2)}) async-start(bf16[16,12,24,128]{3,2,1,0:T(8,128)(2,1)} %bitcast.3), calls=%async_computation.1 | async-start | bytes 2359296 | tf_op jit(solution)/shard_map/all_to_all | solution.py:161
  143.3 18.1 %copy-start.6 = (bf16[16,12,24,128]{3,2,1,0:T(8,128)(2,1)S(1)}, bf16[16,12,24,128]{3,2,1,0:T(8,128)(2,1)}, u32[]{:S(2)}) copy-start(bf16[16,12,24,128]{3,2,1,0:T(8,128)(2,1)} %get-tuple-element.10) | copy-start | bytes 3538948
  234.9 32.5 %all-to-all-start.2 = ((bf16[16,12,24,128]{3,2,1,0:T(8,128)(2,1)}), bf16[16,12,24,128]{3,2,1,0:T(8,128)(2,1)}, u32[]{:S(2)}, u32[]{:S(2)}) async-start(bf16[16,12,24,128]{3,2,1,0:T(8,128)(2,1)} %get-tuple-element.9), calls=%async_computation.2 | async-start | bytes 2359296 | tf_op jit(solution)/shard_map/all_to_all | solution.py:164
  240.5 3.8 %copy-start.8 = (f32[24,192]{1,0:T(8,128)S(1)}, f32[24,192]{1,0:T(8,128)}, u32[]{:S(2)}) copy-start(f32[24,192]{1,0:T(8,128)} %copy-done.7) | copy-start | bytes 55300
  240.5 3.8 %copy-start.12 = (f32[24,192]{1,0:T(8,128)S(1)}, f32[24,192]{1,0:T(8,128)}, u32[]{:S(2)}) copy-start(f32[24,192]{1,0:T(8,128)} %copy-done.11) | copy-start | bytes 55300
  240.5 3.8 %copy-start.19 = (f32[128]{0:T(128)S(1)}, f32[128]{0:T(128)}, u32[]{:S(2)}) copy-start(f32[128]{0:T(128)} %param.7) | copy-start | bytes 1540
  244.3 1.9 copy-start.4
  244.3 1.9 copy-start.9
  244.3 1.9 copy-start.13
  244.3 1.8 copy-start.20
  269.0 19.7 %all-to-all-start.6 = ((f32[32,25,128]{2,1,0:T(8,128)}), f32[32,25,128]{2,1,0:T(8,128)}, u32[]{:S(2)}, u32[]{:S(2)}) async-start(f32[32,25,128]{2,1,0:T(8,128)} %broadcast_in_dim.8), calls=%async_computation.6 | async-start | bytes 1048576 | tf_op jit(solution)/shard_map/all_to_all | solution.py:176
  274.8 2.6 copy-start.16
  274.9 2.6 copy-start.17
  274.9 2.6 copy-start.10
  274.9 2.6 copy-start.14
  (2 other events, 1.7 us)
Sparse Core Ops, SparseCore 0:
  14.8 77.8 all-gather.2
